TPU v7x, 32 devices: a whole 2x2x4 slice. The times are simulated.
32 devices in a mesh: ctx: 8 (over z, y), head: 4 (over x, core).
Axes of the slice: x: 2, y: 2, z: 4, core: 2. Of those that a mesh axis runs over, the one named last changes fastest.
Arguments:
- queries: bfloat16 [4096, 2048], P(('ctx', 'head')), may hold values from -6 to 6
- key_rows: bfloat16 [4096, 256], P(('ctx', 'head')), may hold values from -6 to 6
- value_rows: bfloat16 [4096, 256], P(('ctx', 'head')), may hold values from -8 to 8
- group_kv_head: int32 [4], replicated, may hold values from 0 to 1, as said below
- doc_ids: int32 [4096], replicated, may hold values from 0 to 127, never falling along the last dimension, each value on 1 to 64 neighbouring positions
Outputs:
- attended: bfloat16 [4096, 2048], P(('ctx', 'head'))
Inputs may be any that keep to these rules, and one draw needn't show every extreme that they name: `group_kv_head`: each key-value head is named by exactly two groups. `doc_ids`: ids never fall along the sequence and every id appears; a document holds at most 64 tokens, and one holds exactly that many.
All inputs are finite; a program needn't handle non-finite values.
Results may differ from a plain program's by a relative error of at most 0.0027.
Values may be sent and summed in bfloat16 or wider, within the bound.
No kernel may reach another device: no remote copies, remote signals or barrier semaphores. Data moves between devices by JAX's collectives and lax.ppermute only.
A program may use at most 64 MiB of HBM per device.

v0:
```python
import math
import jax
import jax.numpy as jnp
from jax import lax
from jax.sharding import PartitionSpec as P

HEAD_DIM = 128
HEADS_DEV = 4
neg_fill = -1e30


def passed_along(array, axis, by):
    peers = lax.axis_size(axis)
    pairs = [(i, i + by) for i in range(peers) if 0 <= i + by < peers]
    return lax.ppermute(array, axis, pairs)


def from_partner(array, axis, stride):
    return lax.ppermute(array, axis, [(i, i ^ 1 << stride) for i in range(lax.axis_size(axis))])


def attend(query_tile, key_window, value_window, query_pos, query_doc, key_pos, key_doc):
    scale_factor = 1.0 / math.sqrt(query_tile.shape[3])
    visible = (key_pos[:, None, :] <= query_pos[:, :, None]) & (
        key_doc[:, None, :] == query_doc[:, :, None]
    )
    results = []
    for head_index in range(query_tile.shape[2]):
        scores = (
            jnp.einsum(
                "nhs,nos->nho",
                query_tile[:, :, head_index],
                key_window,
                preferred_element_type=jnp.float32,
            )
            * scale_factor
        )
        scores = jnp.where(visible, scores, neg_fill)
        peak = jnp.max(scores, axis=2, keepdims=True)
        expo = jnp.where(visible, jnp.exp(scores - peak), 0.0)
        totals = jnp.sum(expo, axis=2, keepdims=True)
        mixed = jnp.einsum(
            "fkm,fmp->fkp",
            expo.astype(jnp.bfloat16),
            value_window,
            preferred_element_type=jnp.float32,
        )
        results.append((mixed / totals).astype(jnp.bfloat16))
    return jnp.concatenate(results, axis=2)


def three_tiles(values, tile_count, tile):
    stacked = values.reshape((tile_count + 2, tile) + values.shape[1:])
    return jnp.concatenate([stacked[:tile_count], stacked[1 : tile_count + 1], stacked[2:]], axis=1)


def on_device(queries, key_rows, value_rows, group_kv_head, doc_ids):
    head_count = lax.axis_size("head")
    local_rows = queries.shape[0]
    kv_count = key_rows.shape[1] // HEAD_DIM
    width = HEADS_DEV * HEAD_DIM
    half_dim = HEAD_DIM // 2
    grouped = queries.reshape(local_rows, head_count, width)
    key_split = key_rows.reshape(local_rows, kv_count, HEAD_DIM)
    value_split = value_rows.reshape(local_rows, kv_count, HEAD_DIM)
    tok_dev = local_rows * head_count
    reach = tok_dev // 8
    tile = tok_dev // 16
    tile_count = 16
    order = jnp.argsort(group_kv_head, stable=True)
    reorder = (order[:, None] == jnp.arange(head_count, dtype=jnp.int32)[None, :]).astype(
        jnp.bfloat16
    )
    grouped = jnp.einsum(
        "sg,rgw->rsw", reorder, grouped, preferred_element_type=jnp.float32
    ).astype(jnp.bfloat16)
    key_parts = key_split.reshape(local_rows, kv_count * 2, half_dim)
    value_parts = value_split.reshape(local_rows, kv_count * 2, half_dim)
    pieces = jnp.concatenate([key_parts, value_parts], axis=2)
    local_queries, local_pieces = (
        lax.all_to_all(grouped, "head", split_axis=1, concat_axis=0, tiled=True),
        lax.all_to_all(pieces, "head", split_axis=1, concat_axis=0, tiled=True),
    )
    own_pieces = local_pieces.reshape(tok_dev, HEAD_DIM)
    rim = passed_along(own_pieces[tok_dev - reach :], "ctx", 1)
    mine = jnp.concatenate([rim, own_pieces], axis=0)
    partner = from_partner(mine, "head", 0)
    lower = lax.axis_index("head") % 2 == 0
    own_key = mine[:, :half_dim]
    own_value = mine[:, half_dim:]
    other_key = partner[:, :half_dim]
    other_value = partner[:, half_dim:]
    key_all = jnp.where(
        lower,
        jnp.concatenate([own_key, other_key], axis=1),
        jnp.concatenate([other_key, own_key], axis=1),
    )
    value_all = jnp.where(
        lower,
        jnp.concatenate([own_value, other_value], axis=1),
        jnp.concatenate([other_value, own_value], axis=1),
    )
    query_tiles = local_queries.reshape(tile_count, tile, HEADS_DEV, HEAD_DIM)
    block_start = lax.axis_index("ctx") * tok_dev
    doc_pad = jnp.concatenate([jnp.full((reach,), -1, jnp.int32), doc_ids], axis=0)
    key_doc = lax.dynamic_slice_in_dim(doc_pad, block_start, reach + tok_dev, 0)
    query_doc = lax.dynamic_slice_in_dim(doc_ids, block_start, tok_dev, 0).reshape(tile_count, tile)
    key_pos = block_start - reach + jnp.arange(reach + tok_dev, dtype=jnp.int32)
    query_pos = (block_start + jnp.arange(tok_dev, dtype=jnp.int32)).reshape(tile_count, tile)
    key_windows = three_tiles(key_all, tile_count, tile)
    value_windows = three_tiles(value_all, tile_count, tile)
    key_doc_windows = three_tiles(key_doc, tile_count, tile)
    key_pos_windows = three_tiles(key_pos, tile_count, tile)
    result = attend(
        query_tiles,
        key_windows,
        value_windows,
        query_pos,
        query_doc,
        key_pos_windows,
        key_doc_windows,
    )
    result = result.reshape(tok_dev, 1, width)
    returned = lax.all_to_all(result, "head", split_axis=0, concat_axis=1, tiled=True)
    returned = jnp.einsum(
        "sg,rsw->rgw", reorder, returned, preferred_element_type=jnp.float32
    ).astype(jnp.bfloat16)
    return returned.reshape(local_rows, head_count * width)


def solution(mesh):
    placed = (
        P(("ctx", "head"), None),
        P(("ctx", "head"), None),
        P(("ctx", "head"), None),
        P(),
        P(),
    )
    return jax.shard_map(
        on_device, mesh=mesh, in_specs=placed, out_specs=P(("ctx", "head"), None), check_vma=False
    )
```

profile of v0, /device:TPU:0, one launch (start us, length us, event | category | flops | bytes accessed | tf_op | source)
XLA Modules:
  0.0 51.2 jit_solution(3134931440906846333)
XLA Ops:
  0.0 0.0 copy-start.1
  0.0 0.0 copy-start
  0.0 1.0 %copy.31 = bf16[128,256]{0,1:T(8,128)(2,1)S(1)} copy(bf16[128,256]{1,0:T(8,128)(2,1)} %param.7) | data formatting | bytes 131072 | tf_op args[2]
  1.0 0.0 copy-done.1
  1.0 0.1 copy.30
  1.1 0.7 %pad_maximum_fusion.4 = bf16[128,4,128]{0,2,1:T(8,128)(2,1)} fusion(bf16[128,4,64]{0,2,1:T(8,128)(2,1)S(1)} %bitcast.77, bf16[128,4,64]{0,2,1:T(8,128)(2,1)S(1)} %bitcast.78), kind=kLoop, calls=%fused_computation.48 | loop fusion | flops 262144 | bytes 262144 | tf_op jit(solution)/shard_map/concatenate | solution.py:79
  1.8 4.2 %all-to-all-start.1 = ((bf16[128,4,128]{0,2,1:T(8,128)(2,1)}), bf16[128,4,128]{0,2,1:T(8,128)(2,1)S(1)}, u32[]{:S(2)}, u32[]{:S(2)}) async-start(bf16[128,4,128]{0,2,1:T(8,128)(2,1)} %pad_maximum_fusion.4), calls=%async_computation.1 | async-start | bytes 262144 | tf_op jit(solution)/shard_map/all_to_all | solution.py:82
  6.0 0.0 copy-done
  6.0 0.4 reshape.83
  6.5 0.0 copy-start.3
  6.5 0.6 %copy-done.3 = s32[4]{0:T(128)S(1)} copy-done((s32[4]{0:T(128)S(1)}, s32[4]{0:T(128)}, u32[]{:S(2)}) %copy-start.3) | copy-done | bytes 40
  7.1 0.7 %sort.17 = (s32[4]{0:T(128)}, s32[4]{0:T(128)S(1)}) sort(s32[4]{0:T(128)S(1)} %copy-done.3, s32[4]{0:T(128)S(1)} %iota.54), dimensions={0}, to_apply=%region_0.0 | sort | flops 8 | bytes 64 | tf_op jit(solution)/shard_map/jit(argsort)/sort | solution.py:70
  7.9 0.0 copy-start.2
  7.9 0.5 %fusion.4 = bf16[128,4,512]{2,1,0:T(4,128)(2,1)S(1)} fusion(bf16[128,4,512]{2,1,0:T(4,128)(2,1)S(1)} %reshape.83, s32[4]{0:T(128)S(1)} %get-tuple-element.6), kind=kOutput, calls=%fused_computation.6 | convolution fusion | flops 2359312 | bytes 1048592 | tf_op jit(solution)/shard_map/sg,rgw->rsw/dot_general | solution.py:74
  8.4 0.2 copy-done.2
  8.6 0.1 pad_dynamic-slice_fusion
  8.7 0.1 fusion.51
  8.7 0.9 %copy.28 = bf16[128,4,512]{2,0,1:T(8,128)(2,1)} copy(bf16[128,4,512]{2,1,0:T(4,128)(2,1)S(1)} %fusion.4) | data formatting | bytes 1048576 | tf_op jit(solution)/shard_map/convert_element_type | solution.py:76
  9.6 0.1 slice.128
  9.7 0.1 slice.126
  9.8 0.1 slice.124
  9.8 0.8 %all-to-all-done.1 = bf16[128,4,128]{0,2,1:T(8,128)(2,1)S(1)} async-done(((bf16[128,4,128]{0,2,1:T(8,128)(2,1)}), bf16[128,4,128]{0,2,1:T(8,128)(2,1)S(1)}, u32[]{:S(2)}, u32[]{:S(2)}) %all-to-all-start.1) | async-done | bytes 131104 | tf_op jit(solution)/shard_map/all_to_all | solution.py:82
  10.6 3.5 %all-to-all-start = ((bf16[128,4,512]{2,0,1:T(8,128)(2,1)}), bf16[128,4,512]{2,0,1:T(8,128)(2,1)S(1)}, u32[]{:S(2)}, u32[]{:S(2)}) async-start(bf16[128,4,512]{2,0,1:T(8,128)(2,1)} %copy.28), calls=%async_computation | async-start | bytes 1048576 | tf_op jit(solution)/shard_map/all_to_all | solution.py:81
  14.1 0.1 copy.32
  14.3 4.0 %collective-permute-start = (bf16[64,128]{1,0:T(8,128)(2,1)S(1)}, bf16[64,128]{1,0:T(8,128)(2,1)S(1)}, u32[]{:S(2)}, u32[]{:S(2)}) collective-permute-start(bf16[64,128]{1,0:T(8,128)(2,1)S(1)} %slice.154), channel_id=1, source_target_pairs={{0,4},{4,8},{8,12},{12,16},{16,20},{20,24},{24,28},{1,5},{5,9},{9,... | collective-permute-start | bytes 49160 | tf_op jit(solution)/shard_map/ppermute | solution.py:15
  18.2 0.1 pad_add_fusion
  18.3 1.3 %collective-permute-done = bf16[64,128]{1,0:T(8,128)(2,1)S(1)} collective-permute-done((bf16[64,128]{1,0:T(8,128)(2,1)S(1)}, bf16[64,128]{1,0:T(8,128)(2,1)S(1)}, u32[]{:S(2)}, u32[]{:S(2)}) %collective-permute-start) | collective-permute-done | bytes 16416 | tf_op jit(solution)/shard_map/ppermute | solution.py:15
  19.7 0.1 collective-permute-start.1
  19.8 0.1 dynamic_slice.7
  19.9 0.1 eq.34
  19.9 0.1 fusion.28
  20.1 1.1 %collective-permute-done.1 = bf16[576,128]{1,0:T(8,128)(2,1)S(1)} collective-permute-done((bf16[576,128]{1,0:T(8,128)(2,1)S(1)}, bf16[576,128]{1,0:T(8,128)(2,1)S(1)}, u32[]{:S(2)}, u32[]{:S(2)}) %collective-permute-start.1) | collective-permute-done | bytes 147488 | tf_op jit(solution)/shard_map/ppermute | solution.py:19
  21.1 0.1 fusion.48
  21.2 0.3 maximum_select_fusion
  21.6 0.1 fusion.49
  21.6 0.1 fusion.47
  21.7 1.2 %all-to-all-done = bf16[128,4,512]{2,0,1:T(8,128)(2,1)S(1)} async-done(((bf16[128,4,512]{2,0,1:T(8,128)(2,1)}), bf16[128,4,512]{2,0,1:T(8,128)(2,1)S(1)}, u32[]{:S(2)}, u32[]{:S(2)}) %all-to-all-start) | async-done | bytes 524320 | tf_op jit(solution)/shard_map/all_to_all | solution.py:81
  22.9 0.1 reshape.84
  23.0 1.1 %fusion.46 = (bf16[16,32,1,128]{3,2,1,0:T(2,128)(2,1)S(1)}, bf16[16,32,1,128]{3,2,1,0:T(2,128)(2,1)S(1)}, bf16[16,32,1,128]{3,2,1,0:T(2,128)(2,1)S(1)}, bf16[16,32,1,128]{3,2,1,0:T(2,128)(2,1)S(1)}) fusion(bf16[16,32,4,128]{3,2,1,0:T(4,128)(2,1)S(1)} %reshape.84), kind=kLoop, calls=%fused_computation.74 | loop fusion | bytes 1048576 | tf_op jit(solution)/shard_map/slice | solution.py:32
  24.2 1.4 %fusion.52 = f32[16,32]{1,0:T(8,128)S(1)} fusion(bf16[16,32,1,128]{3,2,1,0:T(2,128)(2,1)S(1)} %get-tuple-element.10, bf16[16,32,128]{2,1,0:T(8,128)(2,1)S(1)} %bitcast.99, bf16[16,32,128]{2,1,0:T(8,128)(2,1)S(1)} %bitcast.107, bf16[16,32,128]{2,1,0:T(8,128)(2,1)S(1)} %bitcast.91, s32[16,32]{1,0:T(8,128)S(1)} %eq.34, s32[16,96]{1,0:T(8,128)S(1)} %get-tuple-element.30, ...), kind=kOutput, calls=%fused_computation.80 | convolution fusion | flops 14303327 | bytes 542720 | tf_op jit(solution)/shard_map/sub | solution.py:40
  25.5 0.5 fusion.9
  26.0 1.4 %fusion.53 = f32[16,32]{1,0:T(8,128)S(1)} fusion(bf16[16,32,1,128]{3,2,1,0:T(2,128)(2,1)S(1)} %get-tuple-element.8, bf16[16,32,128]{2,1,0:T(8,128)(2,1)S(1)} %bitcast.101, bf16[16,32,128]{2,1,0:T(8,128)(2,1)S(1)} %bitcast.109, bf16[16,32,128]{2,1,0:T(8,128)(2,1)S(1)} %bitcast.93, s32[16,32]{1,0:T(8,128)S(1)} %eq.34, s32[16,96]{1,0:T(8,128)S(1)} %get-tuple-element.30, ...), kind=kOutput, calls=%fused_computation.81 | convolution fusion | flops 14303327 | bytes 542720 | tf_op jit(solution)/shard_map/sub | solution.py:40
  27.4 0.5 fusion.10
  27.9 1.4 %fusion.54 = f32[16,32]{1,0:T(8,128)S(1)} fusion(bf16[16,32,1,128]{3,2,1,0:T(2,128)(2,1)S(1)} %get-tuple-element.9, bf16[16,32,128]{2,1,0:T(8,128)(2,1)S(1)} %bitcast.103, bf16[16,32,128]{2,1,0:T(8,128)(2,1)S(1)} %bitcast.111, bf16[16,32,128]{2,1,0:T(8,128)(2,1)S(1)} %bitcast.95, s32[16,32]{1,0:T(8,128)S(1)} %eq.34, s32[16,96]{1,0:T(8,128)S(1)} %get-tuple-element.30, ...), kind=kOutput, calls=%fused_computation.82 | convolution fusion | flops 14303327 | bytes 542720 | tf_op jit(solution)/shard_map/sub | solution.py:40
  29.2 0.5 fusion.11
  29.7 1.4 %fusion.55 = f32[16,32]{1,0:T(8,128)S(1)} fusion(bf16[16,32,1,128]{3,2,1,0:T(2,128)(2,1)S(1)} %get-tuple-element.7, bf16[16,32,128]{2,1,0:T(8,128)(2,1)S(1)} %bitcast.105, bf16[16,32,128]{2,1,0:T(8,128)(2,1)S(1)} %bitcast.113, bf16[16,32,128]{2,1,0:T(8,128)(2,1)S(1)} %bitcast.97, s32[16,32]{1,0:T(8,128)S(1)} %eq.34, s32[16,96]{1,0:T(8,128)S(1)} %get-tuple-element.30, ...), kind=kOutput, calls=%fused_computation.83 | convolution fusion | flops 14303327 | bytes 542720 | tf_op jit(solution)/shard_map/sub | solution.py:40
  31.1 0.5 fusion.12
  31.5 1.1 %fusion.24 = bf16[16,32,128]{2,1,0:T(8,128)(2,1)S(1)} fusion(f32[16,32]{1,0:T(8,128)S(1)} %fusion.52, f32[16,32,96]{2,1,0:T(8,128)S(1)} %fusion.9, bf16[16,32,128]{2,1,0:T(8,128)(2,1)S(1)} %bitcast.83, bf16[16,32,128]{2,1,0:T(8,128)(2,1)S(1)} %bitcast.87, bf16[16,32,128]{2,1,0:T(8,128)(2,1)S(1)} %bitcast.79, s32[16,32]{1,0:T(8,128)S(1)} %eq.34, ...), kind=kOutput, calls=%fused_computation.34 | convolution fusion | flops 14189151 | bytes 739328 | tf_op jit(solution)/shard_map/fkm,fmp->fkp/dot_general | solution.py:42
  32.6 1.1 %fusion.23 = bf16[16,32,128]{2,1,0:T(8,128)(2,1)S(1)} fusion(f32[16,32]{1,0:T(8,128)S(1)} %fusion.53, f32[16,32,96]{2,1,0:T(8,128)S(1)} %fusion.10, bf16[16,32,128]{2,1,0:T(8,128)(2,1)S(1)} %bitcast.84, bf16[16,32,128]{2,1,0:T(8,128)(2,1)S(1)} %bitcast.88, bf16[16,32,128]{2,1,0:T(8,128)(2,1)S(1)} %bitcast.80, s32[16,32]{1,0:T(8,128)S(1)} %eq.34, ...), kind=kOutput, calls=%fused_computation.33 | convolution fusion | flops 14189151 | bytes 739328 | tf_op jit(solution)/shard_map/fkm,fmp->fkp/dot_general | solution.py:42
  33.7 1.1 %fusion.22 = bf16[16,32,128]{2,1,0:T(8,128)(2,1)S(1)} fusion(f32[16,32]{1,0:T(8,128)S(1)} %fusion.54, f32[16,32,96]{2,1,0:T(8,128)S(1)} %fusion.11, bf16[16,32,128]{2,1,0:T(8,128)(2,1)S(1)} %bitcast.85, bf16[16,32,128]{2,1,0:T(8,128)(2,1)S(1)} %bitcast.89, bf16[16,32,128]{2,1,0:T(8,128)(2,1)S(1)} %bitcast.81, s32[16,32]{1,0:T(8,128)S(1)} %eq.34, ...), kind=kOutput, calls=%fused_computation.32 | convolution fusion | flops 14189151 | bytes 739328 | tf_op jit(solution)/shard_map/fkm,fmp->fkp/dot_general | solution.py:42
  34.8 1.1 %fusion.21 = bf16[16,32,128]{2,1,0:T(8,128)(2,1)S(1)} fusion(f32[16,32]{1,0:T(8,128)S(1)} %fusion.55, f32[16,32,96]{2,1,0:T(8,128)S(1)} %fusion.12, bf16[16,32,128]{2,1,0:T(8,128)(2,1)S(1)} %bitcast.86, bf16[16,32,128]{2,1,0:T(8,128)(2,1)S(1)} %bitcast.90, bf16[16,32,128]{2,1,0:T(8,128)(2,1)S(1)} %bitcast.82, s32[16,32]{1,0:T(8,128)S(1)} %eq.34, ...), kind=kOutput, calls=%fused_computation.31 | convolution fusion | flops 14189151 | bytes 739328 | tf_op jit(solution)/shard_map/fkm,fmp->fkp/dot_general | solution.py:42
  35.9 0.1 pad_maximum_fusion
  36.0 0.5 %broadcast.56 = bf16[]{:T(256)} broadcast(bf16[]{:T(256)} %constant.148), dimensions={} | broadcast | bytes 4 | tf_op jit(solution)/shard_map/reshape | solution.py:123
  36.5 1.0 %reduce = bf16[512,512]{1,0:T(8,128)(2,1)S(1)} reduce(bf16[512,1,512]{2,0,1:T(8,128)(2,1)S(1)} %bitcast.70, bf16[]{:T(256)} %broadcast.56), dimensions={1}, to_apply=%copy.36.reduce_sub_computation | reduce | bytes 1048578 | tf_op jit(solution)/shard_map/reshape | solution.py:123
  37.5 0.4 reshape.90
  37.9 11.2 %all_to_all.48 = bf16[4,2,32768]{2,1,0:T(2,128)(2,1)S(1)} all-to-all(bf16[4,2,32768]{2,1,0:T(2,128)(2,1)S(1)} %reshape.90), channel_id=1, replica_groups=mesh['ctx'=8,'head'=4] {'head'}, dimensions={0} | all-to-all | bytes 1048576 | tf_op jit(solution)/shard_map/all_to_all | solution.py:124
  49.1 0.5 %reshape.91 = bf16[512,1,512]{2,1,0:T(2,128)(2,1)S(1)} reshape(bf16[4,2,32768]{2,1,0:T(2,128)(2,1)S(1)} %all_to_all.48) | data formatting | bytes 1048576
  49.6 0.1 copy.40
  49.8 0.5 convolution_convert_fusion
  50.3 0.9 %copy.45 = bf16[16,8,4,512]{3,1,2,0:T(8,128)(2,1)} copy(bf16[16,8,4,512]{3,2,1,0:T(4,128)(2,1)S(1)} %bitcast.75) | data formatting | bytes 1048576
  (6 shorter events, 0.0 us)
Async XLA Ops:
  0.0 1.0 %copy-start.1 = (bf16[128,256]{1,0:T(8,128)(2,1)S(1)}, bf16[128,256]{1,0:T(8,128)(2,1)}, u32[]{:S(2)}) copy-start(bf16[128,256]{1,0:T(8,128)(2,1)} %param.6) | copy-start | bytes 196612
  0.0 6.0 %copy-start = (bf16[128,2048]{1,0:T(8,128)(2,1)S(1)}, bf16[128,2048]{1,0:T(8,128)(2,1)}, u32[]{:S(2)}) copy-start(bf16[128,2048]{1,0:T(8,128)(2,1)} %param.5) | copy-start | bytes 1572868
  1.8 8.8 %all-to-all-start.1 = ((bf16[128,4,128]{0,2,1:T(8,128)(2,1)}), bf16[128,4,128]{0,2,1:T(8,128)(2,1)S(1)}, u32[]{:S(2)}, u32[]{:S(2)}) async-start(bf16[128,4,128]{0,2,1:T(8,128)(2,1)} %pad_maximum_fusion.4), calls=%async_computation.1 | async-start | bytes 262144 | tf_op jit(solution)/shard_map/all_to_all | solution.py:82
  6.5 0.7 %copy-start.3 = (s32[4]{0:T(128)S(1)}, s32[4]{0:T(128)}, u32[]{:S(2)}) copy-start(s32[4]{0:T(128)} %param.8) | copy-start | bytes 52
  7.9 0.7 %copy-start.2 = (s32[4096]{0:T(1024)S(1)}, s32[4096]{0:T(1024)}, u32[]{:S(2)}) copy-start(s32[4096]{0:T(1024)} %param.9) | copy-start | bytes 49156
  10.6 12.3 %all-to-all-start = ((bf16[128,4,512]{2,0,1:T(8,128)(2,1)}), bf16[128,4,512]{2,0,1:T(8,128)(2,1)S(1)}, u32[]{:S(2)}, u32[]{:S(2)}) async-start(bf16[128,4,512]{2,0,1:T(8,128)(2,1)} %copy.28), calls=%async_computation | async-start | bytes 1048576 | tf_op jit(solution)/shard_map/all_to_all | solution.py:81
  14.3 5.4 %collective-permute-start = (bf16[64,128]{1,0:T(8,128)(2,1)S(1)}, bf16[64,128]{1,0:T(8,128)(2,1)S(1)}, u32[]{:S(2)}, u32[]{:S(2)}) collective-permute-start(bf16[64,128]{1,0:T(8,128)(2,1)S(1)} %slice.154), channel_id=1, source_target_pairs={{0,4},{4,8},{8,12},{12,16},{16,20},{20,24},{24,28},{1,5},{5,9},{9,... | collective-permute-start | bytes 49160 | tf_op jit(solution)/shard_map/ppermute | solution.py:15
  19.7 1.4 %collective-permute-start.1 = (bf16[576,128]{1,0:T(8,128)(2,1)S(1)}, bf16[576,128]{1,0:T(8,128)(2,1)S(1)}, u32[]{:S(2)}, u32[]{:S(2)}) collective-permute-start(bf16[576,128]{1,0:T(8,128)(2,1)S(1)} %pad_maximum_fusion.3), channel_id=1, source_target_pairs={{0,1},{1,0},{2,3},{3,2},{4,5},{5,4},{6,7},{7,6},{8,9},{9,8},{10,11... | collective-permute-start | bytes 442376 | tf_op jit(solution)/shard_map/ppermute | solution.py:19
where the time goes:
time: 51.6 us; the launch traced here: 51.2 us
  matrix products  12.7 us (25%)
  starting transfers between devices  11.7 us (23%)
  blocking collectives  11.2 us (22%)
  local copies, waits for them, and re-layouts  7.82 us (15%)
  waiting for transfers between devices  4.42 us (9%)
  other arithmetic  3.04 us (6%)
    all_to_all x1, blocking collectives, on_device(): lax.all_to_all(result, 'head', split_axis=0, concat_axis=1, tiled=True)  11.2 us
    sub x4, matrix products, attend(): expo = jnp.where(visible, jnp.exp(scores - peak), 0.0)  5.47 us
    dot_general x4, matrix products, attend(): jnp.einsum('fkm,fmp->fkp', expo.astype(jnp.bfloat16), value_window, prefe...  4.35 us
    all_to_all x1, starting transfers between devices, on_device(): lax.all_to_all(pieces, 'head', split_axis=1, concat_axis=0, tiled=True)  4.24 us
    ppermute x1, starting transfers between devices, passed_along(): return lax.ppermute(array, axis, pairs)  3.96 us
    unnamed x14, local copies, waits for them, and re-layouts  3.88 us
    all_to_all x1, starting transfers between devices, on_device(): lax.all_to_all(grouped, 'head', split_axis=1, concat_axis=0, tiled=True)  3.47 us
    dot_general x4, matrix products, attend(): jnp.einsum('nhs,nos->nho', query_tile[:, :, head_index], key_window, pref...  1.84 us
  transfers between devices with their start and end apart: 4, of which 4 were waited for; matrix products, arithmetic and copies ran while one was open for 8% of the time, Pallas kernels for 0%

commit v1 on v0

--- a/solution.py
+++ b/solution.py
@@ -121,7 +121,10 @@
         key_doc_windows,
     )
     result = result.reshape(tok_dev, 1, width)
-    returned = lax.all_to_all(result, "head", split_axis=0, concat_axis=1, tiled=True)
+    returned = jnp.concatenate(
+        lax.all_to_all(jnp.stack(jnp.split(result, lax.axis_size("head"), axis=0)), "head", 0, 0),
+        axis=1,
+    )
     returned = jnp.einsum(
         "sg,rsw->rgw", reorder, returned, preferred_element_type=jnp.float32
     ).astype(jnp.bfloat16)

time: 51.6 us -> 49.1 us (0.952)
  local copies, waits for them, and re-layouts: 7.82 us -> 6.32 us
  other arithmetic: 3.04 us -> 2.08 us
    reshape x1 -> x0, other arithmetic: 1.03 us -> none  [on_device(): result = result.reshape(tok_dev, 1, width)]
    unnamed x14 -> x11, local copies, waits for them, and re-layouts: 3.88 us -> 2.86 us
where the time goes in v1:
time: 49.1 us; the launch traced here: 48.7 us
  matrix products  12.7 us (26%)
  starting transfers between devices  11.7 us (24%)
  blocking collectives  11.2 us (23%)
  local copies, waits for them, and re-layouts  6.32 us (13%)
  waiting for transfers between devices  4.42 us (9%)
  other arithmetic  2.08 us (4%)
    all_to_all x1, blocking collectives, on_device(): lax.all_to_all(jnp.stack(jnp.split(result, lax.axis_size('head'), axis=0)...  11.2 us
    sub x4, matrix products, attend(): expo = jnp.where(visible, jnp.exp(scores - peak), 0.0)  5.47 us
    dot_general x4, matrix products, attend(): jnp.einsum('fkm,fmp->fkp', expo.astype(jnp.bfloat16), value_window, prefe...  4.35 us
    all_to_all x1, starting transfers between devices, on_device(): lax.all_to_all(pieces, 'head', split_axis=1, concat_axis=0, tiled=True)  4.24 us
    ppermute x1, starting transfers between devices, passed_along(): return lax.ppermute(array, axis, pairs)  3.96 us
    all_to_all x1, starting transfers between devices, on_device(): lax.all_to_all(grouped, 'head', split_axis=1, concat_axis=0, tiled=True)  3.47 us
    unnamed x11, local copies, waits for them, and re-layouts  2.86 us
    dot_general x4, matrix products, attend(): jnp.einsum('nhs,nos->nho', query_tile[:, :, head_index], key_window, pref...  1.84 us
  transfers between devices with their start and end apart: 4, of which 4 were waited for; matrix products, arithmetic and copies ran while one was open for 8% of the time, Pallas kernels for 0%

profile of v1, /device:TPU:0, one launch (start us, length us, event | category | flops | bytes accessed | tf_op | source)
XLA Modules:
  0.0 48.7 jit_solution(7025890999256477015)
XLA Ops:
  0.0 0.0 copy-start.1
  0.0 0.0 copy-start
  0.0 1.0 %copy.41 = bf16[128,256]{0,1:T(8,128)(2,1)S(1)} copy(bf16[128,256]{1,0:T(8,128)(2,1)} %param.7) | data formatting | bytes 131072 | tf_op args[2]
  1.0 0.0 copy-done.1
  1.0 0.1 copy.40
  1.1 0.7 %pad_maximum_fusion.5 = bf16[128,4,128]{0,2,1:T(8,128)(2,1)} fusion(bf16[128,4,64]{0,2,1:T(8,128)(2,1)S(1)} %bitcast.81, bf16[128,4,64]{0,2,1:T(8,128)(2,1)S(1)} %bitcast.82), kind=kLoop, calls=%fused_computation.49 | loop fusion | flops 262144 | bytes 262144 | tf_op jit(solution)/shard_map/concatenate | solution.py:79
  1.8 4.2 %all-to-all-start.1 = ((bf16[128,4,128]{0,2,1:T(8,128)(2,1)}), bf16[128,4,128]{0,2,1:T(8,128)(2,1)S(1)}, u32[]{:S(2)}, u32[]{:S(2)}) async-start(bf16[128,4,128]{0,2,1:T(8,128)(2,1)} %pad_maximum_fusion.5), calls=%async_computation.1 | async-start | bytes 262144 | tf_op jit(solution)/shard_map/all_to_all | solution.py:82
  6.0 0.0 copy-done
  6.0 0.4 reshape.95
  6.5 0.0 copy-start.3
  6.5 0.6 %copy-done.3 = s32[4]{0:T(128)S(1)} copy-done((s32[4]{0:T(128)S(1)}, s32[4]{0:T(128)}, u32[]{:S(2)}) %copy-start.3) | copy-done | bytes 40
  7.1 0.7 %sort.17 = (s32[4]{0:T(128)}, s32[4]{0:T(128)S(1)}) sort(s32[4]{0:T(128)S(1)} %copy-done.3, s32[4]{0:T(128)S(1)} %iota.54), dimensions={0}, to_apply=%region_0.0 | sort | flops 8 | bytes 64 | tf_op jit(solution)/shard_map/jit(argsort)/sort | solution.py:70
  7.9 0.0 copy-start.2
  7.9 0.5 %fusion.4 = bf16[128,4,512]{2,1,0:T(4,128)(2,1)S(1)} fusion(bf16[128,4,512]{2,1,0:T(4,128)(2,1)S(1)} %reshape.95, s32[4]{0:T(128)S(1)} %get-tuple-element.6), kind=kOutput, calls=%fused_computation.6 | convolution fusion | flops 2359312 | bytes 1048592 | tf_op jit(solution)/shard_map/sg,rgw->rsw/dot_general | solution.py:74
  8.4 0.2 copy-done.2
  8.6 0.1 pad_dynamic-slice_fusion
  8.7 0.1 fusion.52
  8.7 0.9 %copy.38 = bf16[128,4,512]{2,0,1:T(8,128)(2,1)} copy(bf16[128,4,512]{2,1,0:T(4,128)(2,1)S(1)} %fusion.4) | data formatting | bytes 1048576 | tf_op jit(solution)/shard_map/convert_element_type | solution.py:76
  9.6 0.1 slice.132
  9.7 0.1 slice.130
  9.8 0.1 slice.128
  9.8 0.8 %all-to-all-done.1 = bf16[128,4,128]{0,2,1:T(8,128)(2,1)S(1)} async-done(((bf16[128,4,128]{0,2,1:T(8,128)(2,1)}), bf16[128,4,128]{0,2,1:T(8,128)(2,1)S(1)}, u32[]{:S(2)}, u32[]{:S(2)}) %all-to-all-start.1) | async-done | bytes 131104 | tf_op jit(solution)/shard_map/all_to_all | solution.py:82
  10.6 3.5 %all-to-all-start = ((bf16[128,4,512]{2,0,1:T(8,128)(2,1)}), bf16[128,4,512]{2,0,1:T(8,128)(2,1)S(1)}, u32[]{:S(2)}, u32[]{:S(2)}) async-start(bf16[128,4,512]{2,0,1:T(8,128)(2,1)} %copy.38), calls=%async_computation | async-start | bytes 1048576 | tf_op jit(solution)/shard_map/all_to_all | solution.py:81
  14.1 0.1 copy.42
  14.3 4.0 %collective-permute-start = (bf16[64,128]{1,0:T(8,128)(2,1)S(1)}, bf16[64,128]{1,0:T(8,128)(2,1)S(1)}, u32[]{:S(2)}, u32[]{:S(2)}) collective-permute-start(bf16[64,128]{1,0:T(8,128)(2,1)S(1)} %slice.158), channel_id=1, source_target_pairs={{0,4},{4,8},{8,12},{12,16},{16,20},{20,24},{24,28},{1,5},{5,9},{9,... | collective-permute-start | bytes 49160 | tf_op jit(solution)/shard_map/ppermute | solution.py:15
  18.2 0.1 pad_add_fusion
  18.3 1.3 %collective-permute-done = bf16[64,128]{1,0:T(8,128)(2,1)S(1)} collective-permute-done((bf16[64,128]{1,0:T(8,128)(2,1)S(1)}, bf16[64,128]{1,0:T(8,128)(2,1)S(1)}, u32[]{:S(2)}, u32[]{:S(2)}) %collective-permute-start) | collective-permute-done | bytes 16416 | tf_op jit(solution)/shard_map/ppermute | solution.py:15
  19.7 0.1 collective-permute-start.1
  19.8 0.1 dynamic_slice.7
  19.9 0.1 eq.34
  19.9 0.1 fusion.28
  20.1 1.1 %collective-permute-done.1 = bf16[576,128]{1,0:T(8,128)(2,1)S(1)} collective-permute-done((bf16[576,128]{1,0:T(8,128)(2,1)S(1)}, bf16[576,128]{1,0:T(8,128)(2,1)S(1)}, u32[]{:S(2)}, u32[]{:S(2)}) %collective-permute-start.1) | collective-permute-done | bytes 147488 | tf_op jit(solution)/shard_map/ppermute | solution.py:19
  21.1 0.1 fusion.49
  21.2 0.3 maximum_select_fusion
  21.6 0.1 fusion.50
  21.6 0.1 fusion.48
  21.7 1.2 %all-to-all-done = bf16[128,4,512]{2,0,1:T(8,128)(2,1)S(1)} async-done(((bf16[128,4,512]{2,0,1:T(8,128)(2,1)}), bf16[128,4,512]{2,0,1:T(8,128)(2,1)S(1)}, u32[]{:S(2)}, u32[]{:S(2)}) %all-to-all-start) | async-done | bytes 524320 | tf_op jit(solution)/shard_map/all_to_all | solution.py:81
  22.9 0.1 reshape.96
  23.0 1.1 %fusion.47 = (bf16[16,32,1,128]{3,2,1,0:T(2,128)(2,1)S(1)}, bf16[16,32,1,128]{3,2,1,0:T(2,128)(2,1)S(1)}, bf16[16,32,1,128]{3,2,1,0:T(2,128)(2,1)S(1)}, bf16[16,32,1,128]{3,2,1,0:T(2,128)(2,1)S(1)}) fusion(bf16[16,32,4,128]{3,2,1,0:T(4,128)(2,1)S(1)} %reshape.96), kind=kLoop, calls=%fused_computation.76 | loop fusion | bytes 1048576 | tf_op jit(solution)/shard_map/slice | solution.py:32
  24.2 1.4 %fusion.53 = f32[16,32]{1,0:T(8,128)S(1)} fusion(bf16[16,32,1,128]{3,2,1,0:T(2,128)(2,1)S(1)} %get-tuple-element.14, bf16[16,32,128]{2,1,0:T(8,128)(2,1)S(1)} %bitcast.103, bf16[16,32,128]{2,1,0:T(8,128)(2,1)S(1)} %bitcast.111, bf16[16,32,128]{2,1,0:T(8,128)(2,1)S(1)} %bitcast.95, s32[16,32]{1,0:T(8,128)S(1)} %eq.34, s32[16,96]{1,0:T(8,128)S(1)} %get-tuple-element.34, ...), kind=kOutput, calls=%fused_computation.82 | convolution fusion | flops 14303327 | bytes 542720 | tf_op jit(solution)/shard_map/sub | solution.py:40
  25.5 0.5 fusion.9
  26.0 1.4 %fusion.54 = f32[16,32]{1,0:T(8,128)S(1)} fusion(bf16[16,32,1,128]{3,2,1,0:T(2,128)(2,1)S(1)} %get-tuple-element.12, bf16[16,32,128]{2,1,0:T(8,128)(2,1)S(1)} %bitcast.105, bf16[16,32,128]{2,1,0:T(8,128)(2,1)S(1)} %bitcast.113, bf16[16,32,128]{2,1,0:T(8,128)(2,1)S(1)} %bitcast.97, s32[16,32]{1,0:T(8,128)S(1)} %eq.34, s32[16,96]{1,0:T(8,128)S(1)} %get-tuple-element.34, ...), kind=kOutput, calls=%fused_computation.83 | convolution fusion | flops 14303327 | bytes 542720 | tf_op jit(solution)/shard_map/sub | solution.py:40
  27.4 0.5 fusion.10
  27.9 1.4 %fusion.55 = f32[16,32]{1,0:T(8,128)S(1)} fusion(bf16[16,32,1,128]{3,2,1,0:T(2,128)(2,1)S(1)} %get-tuple-element.13, bf16[16,32,128]{2,1,0:T(8,128)(2,1)S(1)} %bitcast.107, bf16[16,32,128]{2,1,0:T(8,128)(2,1)S(1)} %bitcast.115, bf16[16,32,128]{2,1,0:T(8,128)(2,1)S(1)} %bitcast.99, s32[16,32]{1,0:T(8,128)S(1)} %eq.34, s32[16,96]{1,0:T(8,128)S(1)} %get-tuple-element.34, ...), kind=kOutput, calls=%fused_computation.84 | convolution fusion | flops 14303327 | bytes 542720 | tf_op jit(solution)/shard_map/sub | solution.py:40
  29.2 0.5 fusion.11
  29.7 1.4 %fusion.56 = f32[16,32]{1,0:T(8,128)S(1)} fusion(bf16[16,32,1,128]{3,2,1,0:T(2,128)(2,1)S(1)} %get-tuple-element.11, bf16[16,32,128]{2,1,0:T(8,128)(2,1)S(1)} %bitcast.109, bf16[16,32,128]{2,1,0:T(8,128)(2,1)S(1)} %bitcast.117, bf16[16,32,128]{2,1,0:T(8,128)(2,1)S(1)} %bitcast.101, s32[16,32]{1,0:T(8,128)S(1)} %eq.34, s32[16,96]{1,0:T(8,128)S(1)} %get-tuple-element.34, ...), kind=kOutput, calls=%fused_computation.85 | convolution fusion | flops 14303327 | bytes 542720 | tf_op jit(solution)/shard_map/sub | solution.py:40
  31.1 0.5 fusion.12
  31.5 1.1 %fusion.24 = bf16[16,32,128]{2,1,0:T(8,128)(2,1)S(1)} fusion(f32[16,32]{1,0:T(8,128)S(1)} %fusion.53, f32[16,32,96]{2,1,0:T(8,128)S(1)} %fusion.9, bf16[16,32,128]{2,1,0:T(8,128)(2,1)S(1)} %bitcast.87, bf16[16,32,128]{2,1,0:T(8,128)(2,1)S(1)} %bitcast.91, bf16[16,32,128]{2,1,0:T(8,128)(2,1)S(1)} %bitcast.83, s32[16,32]{1,0:T(8,128)S(1)} %eq.34, ...), kind=kOutput, calls=%fused_computation.34 | convolution fusion | flops 14189151 | bytes 739328 | tf_op jit(solution)/shard_map/fkm,fmp->fkp/dot_general | solution.py:42
  32.6 1.1 %fusion.23 = bf16[16,32,128]{2,1,0:T(8,128)(2,1)S(1)} fusion(f32[16,32]{1,0:T(8,128)S(1)} %fusion.54, f32[16,32,96]{2,1,0:T(8,128)S(1)} %fusion.10, bf16[16,32,128]{2,1,0:T(8,128)(2,1)S(1)} %bitcast.88, bf16[16,32,128]{2,1,0:T(8,128)(2,1)S(1)} %bitcast.92, bf16[16,32,128]{2,1,0:T(8,128)(2,1)S(1)} %bitcast.84, s32[16,32]{1,0:T(8,128)S(1)} %eq.34, ...), kind=kOutput, calls=%fused_computation.33 | convolution fusion | flops 14189151 | bytes 739328 | tf_op jit(solution)/shard_map/fkm,fmp->fkp/dot_general | solution.py:42
  33.7 1.1 %fusion.22 = bf16[16,32,128]{2,1,0:T(8,128)(2,1)S(1)} fusion(f32[16,32]{1,0:T(8,128)S(1)} %fusion.55, f32[16,32,96]{2,1,0:T(8,128)S(1)} %fusion.11, bf16[16,32,128]{2,1,0:T(8,128)(2,1)S(1)} %bitcast.89, bf16[16,32,128]{2,1,0:T(8,128)(2,1)S(1)} %bitcast.93, bf16[16,32,128]{2,1,0:T(8,128)(2,1)S(1)} %bitcast.85, s32[16,32]{1,0:T(8,128)S(1)} %eq.34, ...), kind=kOutput, calls=%fused_computation.32 | convolution fusion | flops 14189151 | bytes 739328 | tf_op jit(solution)/shard_map/fkm,fmp->fkp/dot_general | solution.py:42
  34.8 1.1 %fusion.21 = bf16[16,32,128]{2,1,0:T(8,128)(2,1)S(1)} fusion(f32[16,32]{1,0:T(8,128)S(1)} %fusion.56, f32[16,32,96]{2,1,0:T(8,128)S(1)} %fusion.12, bf16[16,32,128]{2,1,0:T(8,128)(2,1)S(1)} %bitcast.90, bf16[16,32,128]{2,1,0:T(8,128)(2,1)S(1)} %bitcast.94, bf16[16,32,128]{2,1,0:T(8,128)(2,1)S(1)} %bitcast.86, s32[16,32]{1,0:T(8,128)S(1)} %eq.34, ...), kind=kOutput, calls=%fused_computation.31 | convolution fusion | flops 14189151 | bytes 739328 | tf_op jit(solution)/shard_map/fkm,fmp->fkp/dot_general | solution.py:42
  35.9 0.1 pad_maximum_fusion
  36.0 0.1 pad_maximum_fusion.1
  36.1 11.2 %all_to_all.35 = bf16[4,128,1,512]{3,1,2,0:T(8,128)(2,1)S(1)} all-to-all(bf16[4,128,1,512]{3,1,2,0:T(8,128)(2,1)S(1)} %pad_maximum_fusion.1), channel_id=1, replica_groups=mesh['ctx'=8,'head'=4] {'head'}, dimensions={0} | all-to-all | bytes 1048576 | tf_op jit(solution)/shard_map/all_to_all | solution.py:125
  47.3 0.5 %convolution_convert_fusion = bf16[128,512,4]{1,2,0:T(4,128)(2,1)S(1)} fusion(bf16[4,128,1,512]{3,1,2,0:T(8,128)(2,1)S(1)} %all_to_all.35, s32[4]{0:T(128)S(1)} %get-tuple-element.6), kind=kOutput, calls=%fused_computation.4 | convolution fusion | flops 2359312 | bytes 1048592 | tf_op jit(solution)/shard_map/sg,rsw->rgw/dot_general | solution.py:128
  47.8 0.9 %copy.53 = bf16[16,8,4,512]{3,1,2,0:T(8,128)(2,1)} copy(bf16[16,8,4,512]{3,2,1,0:T(4,128)(2,1)S(1)} %bitcast.75) | data formatting | bytes 1048576
  (7 shorter events, 0.1 us)
Async XLA Ops:
  0.0 1.0 %copy-start.1 = (bf16[128,256]{1,0:T(8,128)(2,1)S(1)}, bf16[128,256]{1,0:T(8,128)(2,1)}, u32[]{:S(2)}) copy-start(bf16[128,256]{1,0:T(8,128)(2,1)} %param.6) | copy-start | bytes 196612
  0.0 6.0 %copy-start = (bf16[128,2048]{1,0:T(8,128)(2,1)S(1)}, bf16[128,2048]{1,0:T(8,128)(2,1)}, u32[]{:S(2)}) copy-start(bf16[128,2048]{1,0:T(8,128)(2,1)} %param.5) | copy-start | bytes 1572868
  1.8 8.8 %all-to-all-start.1 = ((bf16[128,4,128]{0,2,1:T(8,128)(2,1)}), bf16[128,4,128]{0,2,1:T(8,128)(2,1)S(1)}, u32[]{:S(2)}, u32[]{:S(2)}) async-start(bf16[128,4,128]{0,2,1:T(8,128)(2,1)} %pad_maximum_fusion.5), calls=%async_computation.1 | async-start | bytes 262144 | tf_op jit(solution)/shard_map/all_to_all | solution.py:82
  6.5 0.7 %copy-start.3 = (s32[4]{0:T(128)S(1)}, s32[4]{0:T(128)}, u32[]{:S(2)}) copy-start(s32[4]{0:T(128)} %param.8) | copy-start | bytes 52
  7.9 0.7 %copy-start.2 = (s32[4096]{0:T(1024)S(1)}, s32[4096]{0:T(1024)}, u32[]{:S(2)}) copy-start(s32[4096]{0:T(1024)} %param.9) | copy-start | bytes 49156
  10.6 12.3 %all-to-all-start = ((bf16[128,4,512]{2,0,1:T(8,128)(2,1)}), bf16[128,4,512]{2,0,1:T(8,128)(2,1)S(1)}, u32[]{:S(2)}, u32[]{:S(2)}) async-start(bf16[128,4,512]{2,0,1:T(8,128)(2,1)} %copy.38), calls=%async_computation | async-start | bytes 1048576 | tf_op jit(solution)/shard_map/all_to_all | solution.py:81
  14.3 5.4 %collective-permute-start = (bf16[64,128]{1,0:T(8,128)(2,1)S(1)}, bf16[64,128]{1,0:T(8,128)(2,1)S(1)}, u32[]{:S(2)}, u32[]{:S(2)}) collective-permute-start(bf16[64,128]{1,0:T(8,128)(2,1)S(1)} %slice.158), channel_id=1, source_target_pairs={{0,4},{4,8},{8,12},{12,16},{16,20},{20,24},{24,28},{1,5},{5,9},{9,... | collective-permute-start | bytes 49160 | tf_op jit(solution)/shard_map/ppermute | solution.py:15
  19.7 1.4 %collective-permute-start.1 = (bf16[576,128]{1,0:T(8,128)(2,1)S(1)}, bf16[576,128]{1,0:T(8,128)(2,1)S(1)}, u32[]{:S(2)}, u32[]{:S(2)}) collective-permute-start(bf16[576,128]{1,0:T(8,128)(2,1)S(1)} %pad_maximum_fusion.4), channel_id=1, source_target_pairs={{0,1},{1,0},{2,3},{3,2},{4,5},{5,4},{6,7},{7,6},{8,9},{9,8},{10,11... | collective-permute-start | bytes 442376 | tf_op jit(solution)/shard_map/ppermute | solution.py:19
